TPU v7x, 256 devices: a whole 4x4x8 slice. The times are simulated.
256 devices in a mesh: path: 32 (over x, z), mp: 2 (over core), period: 4 (over y).
Axes of the slice: x: 4, y: 4, z: 8, core: 2. Of those that a mesh axis runs over, the one named last changes fastest.
Arguments:
- tiles: bfloat16 [4096, 256, 256], P(('path', 'mp')), may hold values from -0.375 to 0.375
- tile_rows: int32 [4096], P(('path', 'mp')), may hold values from 0 to 7
- tile_cols: int32 [4096], P(('path', 'mp')), may hold values from 0 to 1023, as said below
- tile_counts: int32 [64], P(('path', 'mp')), may hold values from 8 to 64, as said below
- data: float32 [262144], P(('period', 'path')), parts along dimension 0, may hold values from -6 to 6
Outputs:
- solution: float32 [2097152], P(('period', 'path', 'mp')), parts along dimension 0
- left_vector: float32 [262144], P(('period', 'path')), parts along dimension 0
There are 4 independent parts, one for each index of `period`. A program takes and returns all parts, laid end to end along the dimension named above; an argument that names none is the same for every part. Nothing has to cross between parts.
Inputs may be any that keep to these rules, and one draw needn't show every extreme that they name: `tile_counts`: slots from the strip's count on are unused; some strips are full. `tile_cols`: among all 64 slots of one strip, at most 8 name cell tiles t with the same t // 32, and in every strip some value of t // 32 is named by exactly 8 slots.
All inputs are finite; a program needn't handle non-finite values.
Results may differ from a plain program's by a relative error of at most 0.0066.
Values may be sent and summed in bfloat16 or wider, within the bound.
No kernel may reach another device: no remote copies, remote signals or barrier semaphores. Data moves between devices by JAX's collectives and lax.ppermute only.
A program may use at most 64 MiB of HBM per device.

v0:
```python
import jax
import jax.numpy as jnp
from jax import lax
from jax.sharding import PartitionSpec as P

CT_DEV = 32
ITERS = 2


def on_device(tiles, tile_rows, tile_cols, tile_counts, data):
    tile = tiles.shape[1]
    slots = tiles.shape[0]
    row_tiles = data.shape[0] // tile
    npath = lax.axis_size("path")
    half_tiles = CT_DEV * npath
    limit = max(2, max(slots // 8, (slots + npath - 1) // npath))
    live = lax.iota(jnp.int32, slots) < tile_counts[0]
    row_onehot = (
        (tile_rows[None, :] == lax.iota(jnp.int32, row_tiles)[:, None]) & live[None, :]
    ).astype(jnp.float32)
    col_onehot = (
        (tile_cols[None, :] == lax.iota(jnp.int32, half_tiles)[:, None]) & live[None, :]
    ).astype(jnp.float32)
    owner = tile_cols // CT_DEV
    inside = tile_cols % CT_DEV
    same_owner = (owner[:, None] == owner[None, :]).astype(jnp.int32)
    earlier = (lax.iota(jnp.int32, slots)[None, :] < lax.iota(jnp.int32, slots)[:, None]).astype(
        jnp.int32
    )
    rank = jnp.sum(same_owner * earlier, axis=1)
    target = owner * limit + rank
    place = lax.iota(jnp.int32, npath * limit)[:, None] == target[None, :]
    place_live = (place & live[None, :]).astype(jnp.float32)
    slot_inside = (
        jnp.sum(jnp.where(place, inside[None, :], 0), axis=1)
        - 1
        + jnp.sum(place.astype(jnp.int32), axis=1)
    )
    send_index = jnp.where(jnp.sum(place_live, axis=1) > 0, slot_inside, -1).reshape(npath, limit)

    def forward_prods(picked):
        prods = jnp.einsum("sij,sj->si", tiles, picked, preferred_element_type=jnp.float32)
        local = jnp.dot(row_onehot, prods, precision=lax.Precision.HIGHEST).reshape(-1)
        return lax.psum(local, "mp")

    def backward_prods(left_b):
        picked = left_b.reshape(row_tiles, tile)[tile_rows]
        return jnp.einsum("sij,si->sj", tiles, picked, preferred_element_type=jnp.float32)

    def row_norm(left):
        return jnp.sqrt(lax.psum(jnp.sum(left * left), "path") + 1e-12)

    def col_norm(own):
        return jnp.sqrt(lax.psum(jnp.sum(own * own), ("path", "mp")) + 1e-12)

    def right_step(left, state, beta, asked):
        prods = backward_prods(left.astype(jnp.bfloat16))
        partial_cols = jnp.dot(col_onehot, prods, precision=lax.Precision.HIGHEST).reshape(-1)
        own = lax.psum_scatter(partial_cols, "path", scatter_dimension=0, tiled=True)
        if state is not None:
            own = own - beta * state
        alpha = col_norm(own)
        own = own / alpha
        return (own, own, alpha, asked)

    beta = row_norm(data)
    left = data / beta
    phibar = beta
    asked = send_index
    state, right, alpha, asked = right_step(left, None, beta, asked)
    search = right
    rhobar = alpha
    solution = jnp.zeros_like(right)
    for step in range(ITERS):
        half_b = lax.all_gather(state.astype(jnp.bfloat16), "path", axis=0, tiled=True)
        forward_picked = half_b.reshape(half_tiles, tile)[tile_cols]
        left = forward_prods(forward_picked) - alpha * left
        beta = row_norm(left)
        left = left / beta
        state, right, alpha, asked = right_step(left, state, beta, asked)
        rho = jnp.sqrt(rhobar * rhobar + beta * beta)
        cosine = rhobar / rho
        sine = beta / rho
        theta = sine * alpha
        rhobar = -cosine * alpha
        phi = cosine * phibar
        phibar = sine * phibar
        solution = solution + phi / rho * search
        search = right - theta / rho * search
    total_rows = row_tiles * tile * npath
    return (solution, left * jnp.sqrt(jnp.float32(total_rows)))


def solution(mesh):
    placed = (
        P(("path", "mp"), None, None),
        P(("path", "mp")),
        P(("path", "mp")),
        P(("path", "mp")),
        P(("period", "path")),
    )
    return jax.shard_map(
        on_device,
        mesh=mesh,
        in_specs=placed,
        out_specs=(P(("period", "path", "mp")), P(("period", "path"))),
        check_vma=False,
    )
```

profile of v0, /device:TPU:8, one launch (start us, length us, event | category | flops | bytes accessed | tf_op | source)
XLA Modules:
  0.0 916.7 jit_solution(12098558276543920752)
XLA Ops:
  7.2 1.3 multiply_reduce_fusion.4
  8.5 78.3 %psum.49 = f32[]{:T(128)} all-reduce(f32[]{:T(128)} %multiply_reduce_fusion.4), channel_id=1, replica_groups=mesh['path'=32,'mp'=2,'period'=4] {'path'}, use_global_device_ids=true, to_apply=%region_1.0 | all-reduce | flops 1 | bytes 8 | tf_op jit(solution)/shard_map/psum | solution.py:51
  87.5 0.7 fusion.27
  88.2 0.7 compare_select_fusion.1
  89.6 0.7 gather_fusion
  90.3 4.6 fusion.21
  95.4 1.6 copy.15
  98.3 143.1 %all-reduce.5.cloned.1.call-done = f32[262144]{0:T(1024)} async-done(((f32[262144]{0:T(1024)}), f32[262144]{0:T(1024)}) %all-reduce.5.cloned.1.call-update) | async-done | bytes 1048592
  241.5 1.4 multiply_reduce_fusion.1
  242.8 124.7 %psum.50 = f32[]{:T(128)} all-reduce(f32[]{:T(128)} %multiply_reduce_fusion.1), channel_id=1, replica_groups=mesh['path'=32,'mp'=2,'period'=4] {'path','mp'}, use_global_device_ids=true, to_apply=%region_4.0 | all-reduce | flops 1 | bytes 8 | tf_op jit(solution)/shard_map/psum | solution.py:54
  368.2 0.8 fusion.33
  369.0 46.3 %all_gather.6 = bf16[262144]{0:T(1024)(128)(2,1)S(1)} all-gather(bf16[8192]{0:T(1024)(128)(2,1)S(1)} %fusion.33), channel_id=1, replica_groups=mesh['path'=32,'mp'=2,'period'=4] {'path'}, dimensions={0}, use_global_device_ids=true | all-gather | bytes 540672 | tf_op jit(solution)/shard_map/all_gather | solution.py:75
  415.5 0.7 gather_fusion.1
  416.2 5.6 fusion.18
  422.0 2.5 psum.51
  424.5 0.6 multiply_reduce_fusion.3
  425.1 72.9 %psum.52 = f32[]{:T(128)} all-reduce(f32[]{:T(128)} %get-tuple-element.2), channel_id=1, replica_groups=mesh['path'=32,'mp'=2,'period'=4] {'path'}, use_global_device_ids=true, to_apply=%region_7.0 | all-reduce | flops 1 | bytes 8 | tf_op jit(solution)/shard_map/psum | solution.py:51
  498.7 0.7 gather_fusion.2
  499.4 4.6 fusion.15
  504.6 1.5 copy.17
  506.3 144.1 %all-reduce.7.cloned.1.call-done = f32[262144]{0:T(1024)} async-done(((f32[262144]{0:T(1024)}), f32[262144]{0:T(1024)}) %all-reduce.7.cloned.1.call-update) | async-done | bytes 1048592
  650.3 1.4 multiply_reduce_fusion
  651.8 124.7 %psum.53 = f32[]{:T(128)} all-reduce(f32[]{:T(128)} %multiply_reduce_fusion), channel_id=1, replica_groups=mesh['path'=32,'mp'=2,'period'=4] {'path','mp'}, use_global_device_ids=true, to_apply=%region_10.0 | all-reduce | flops 1 | bytes 8 | tf_op jit(solution)/shard_map/psum | solution.py:54
  777.2 0.8 fusion.23
  778.0 46.3 %all_gather.7 = bf16[262144]{0:T(1024)(128)(2,1)S(1)} all-gather(bf16[8192]{0:T(1024)(128)(2,1)S(1)} %fusion.23), channel_id=1, replica_groups=mesh['path'=32,'mp'=2,'period'=4] {'path'}, dimensions={0}, use_global_device_ids=true | all-gather | bytes 540672 | tf_op jit(solution)/shard_map/all_gather | solution.py:75
  824.5 0.7 gather_fusion.3
  825.2 5.6 fusion.12
  831.0 2.5 psum.54
  833.5 0.6 multiply_reduce_fusion.2
  834.1 72.9 %psum.55 = f32[]{:T(128)} all-reduce(f32[]{:T(128)} %multiply_reduce_fusion.2), channel_id=1, replica_groups=mesh['path'=32,'mp'=2,'period'=4] {'path'}, use_global_device_ids=true, to_apply=%region_13.0 | all-reduce | flops 1 | bytes 8 | tf_op jit(solution)/shard_map/psum | solution.py:51
  907.7 0.6 divide_multiply_fusion
  908.5 1.4 multiply_add_fusion
  (28 shorter events, 2.5 us)
Async XLA Ops:
  7.2 87.7 %copy-start.1 = (s32[64]{0:T(128)S(1)}, s32[64]{0:T(128)}, u32[]{:S(2)}) copy-start(s32[64]{0:T(128)} %param.7) | copy-start | bytes 772
  7.2 234.3 %all-reduce.5.cloned.1.call-start = ((), (), s32[]{:S(2)}) async-start(), calls=%async_computation | async-start | bytes 2097152
  90.3 6.8 copy-start.3
  94.9 326.9 %copy-start.2 = (s32[64]{0:T(128)S(1)}, s32[64]{0:T(128)}, u32[]{:S(2)}) copy-start(s32[64]{0:T(128)} %param.6) | copy-start | bytes 772
  94.9 329.6 %copy-start = (f32[2048]{0:T(1024)S(1)}, f32[2048]{0:T(1024)}, u32[]{:S(2)}) copy-start(f32[2048]{0:T(1024)} %param.9) | copy-start | bytes 24580
  97.0 553.3 %all-reduce.7.cloned.1.call-start = ((), (), s32[]{:S(2)}) async-start(), calls=%async_computation.1 | async-start | bytes 2097152
Sparse Core Ops, SparseCore 0:
  97.1 144.2 all-reduce.4
  506.2 144.0 all-reduce.6
where the time goes:
time: 918 us; the launch traced here: 917 us
  blocking collectives  571 us (62%)
  waiting for transfers between devices  287 us (31%)
  matrix products  21.8 us (2%)
  between operations  19.3 us (2%)
  other arithmetic  10.3 us (1%)
    unnamed x4, waiting for transfers between devices  287 us
    psum x2, blocking collectives, col_norm(): return jnp.sqrt(lax.psum(jnp.sum(own * own), ('path', 'mp')) + 1e-12)  249 us
    psum x3, blocking collectives, row_norm(): return jnp.sqrt(lax.psum(jnp.sum(left * left), 'path') + 1e-12)  224 us
    all_gather x2, blocking collectives, on_device(): lax.all_gather(state.astype(jnp.bfloat16), 'path', axis=0, tiled=True)  92.6 us
  transfers between devices with their start and end apart: 2, of which 2 were waited for; matrix products, arithmetic and copies ran while one was open for 0% of the time, Pallas kernels for 0%

commit v1 on v0

--- a/solution.py
+++ b/solution.py
@@ -72,7 +72,12 @@
     rhobar = alpha
     solution = jnp.zeros_like(right)
     for step in range(ITERS):
-        half_b = lax.all_gather(state.astype(jnp.bfloat16), "path", axis=0, tiled=True)
+        half_b = jnp.concatenate(
+            lax.all_to_all(
+                jnp.stack([state.astype(jnp.bfloat16)] * lax.axis_size("path")), "path", 0, 0
+            ),
+            axis=0,
+        )
         forward_picked = half_b.reshape(half_tiles, tile)[tile_cols]
         left = forward_prods(forward_picked) - alpha * left
         beta = row_norm(left)

time: 918 us -> 888 us (0.967)
  blocking collectives: 571 us -> 479 us
  waiting for transfers between devices: 287 us -> 321 us
  other arithmetic: 10.3 us -> 24.5 us
    all_gather x2 -> x0, blocking collectives: 92.6 us -> none  [on_device(): lax.all_gather(state.astype(jnp.bfloat16), 'path', axis=0, tiled=True)]
    all_to_all x0 -> x2, waiting for transfers between devices: none -> 33.6 us  [on_device(): lax.all_to_all(jnp.stack([state.astype(jnp.bfloat16)] * lax.axis_size('pa...]
  transfers between devices with their start and end apart: 2 -> 4, of which waited for: 2 -> 4; matrix products, arithmetic and copies ran while one was open for 0% -> 0% of each run, Pallas kernels for 0% -> 0%
where the time goes in v1:
time: 888 us; the launch traced here: 887 us
  blocking collectives  479 us (54%)
  waiting for transfers between devices  321 us (36%)
  other arithmetic  24.5 us (3%)
  matrix products  21.9 us (2%)
  between operations  19.4 us (2%)
  local copies, waits for them, and re-layouts  12.8 us (1%)
    unnamed x4, waiting for transfers between devices  287 us
    psum x2, blocking collectives, col_norm(): return jnp.sqrt(lax.psum(jnp.sum(own * own), ('path', 'mp')) + 1e-12)  249 us
    psum x3, blocking collectives, row_norm(): return jnp.sqrt(lax.psum(jnp.sum(left * left), 'path') + 1e-12)  225 us
    all_to_all x2, waiting for transfers between devices, on_device(): lax.all_to_all(jnp.stack([state.astype(jnp.bfloat16)] * lax.axis_size('pa...  33.6 us
  transfers between devices with their start and end apart: 4, of which 4 were waited for; matrix products, arithmetic and copies ran while one was open for 0% of the time, Pallas kernels for 0%

profile of v1, /device:TPU:8, one launch (start us, length us, event | category | flops | bytes accessed | tf_op | source)
XLA Modules:
  0.0 886.8 jit_solution(2605861206759245613)
XLA Ops:
  7.2 1.3 multiply_reduce_fusion.4
  8.5 78.3 %psum.49 = f32[]{:T(128)} all-reduce(f32[]{:T(128)} %multiply_reduce_fusion.4), channel_id=1, replica_groups=mesh['path'=32,'mp'=2,'period'=4] {'path'}, use_global_device_ids=true, to_apply=%region_1.0 | all-reduce | flops 1 | bytes 8 | tf_op jit(solution)/shard_map/psum | solution.py:51
  90.3 4.6 fusion.21
  95.4 1.6 copy.15
  98.3 143.1 %all-reduce.5.cloned.1.call-done = f32[262144]{0:T(1024)} async-done(((f32[262144]{0:T(1024)}), f32[262144]{0:T(1024)}) %all-reduce.5.cloned.1.call-update) | async-done | bytes 1048592
  241.4 1.4 multiply_reduce_fusion.1
  242.8 124.7 %psum.50 = f32[]{:T(128)} all-reduce(f32[]{:T(128)} %multiply_reduce_fusion.1), channel_id=1, replica_groups=mesh['path'=32,'mp'=2,'period'=4] {'path','mp'}, use_global_device_ids=true, to_apply=%region_4.0 | all-reduce | flops 1 | bytes 8 | tf_op jit(solution)/shard_map/psum | solution.py:54
  368.9 0.9 stack.4
  370.4 3.8 reduce.2
  374.2 1.2 reshape.98
  375.4 3.9 all-to-all-start
  379.6 16.8 %all-to-all-done = bf16[32,2,4096]{2,1,0:T(2,128)(2,1)S(1)} async-done(((bf16[32,2,4096]{2,1,0:T(2,128)(2,1)}), bf16[32,2,4096]{2,1,0:T(2,128)(2,1)S(1)}, u32[]{:S(2)}, u32[]{:S(2)}) %all-to-all-start) | async-done | bytes 524320 | tf_op jit(solution)/shard_map/all_to_all | solution.py:76
  396.9 3.2 reduce
  401.0 5.6 fusion.18
  406.8 2.5 psum.51
  409.9 73.1 %psum.52 = f32[]{:T(128)} all-reduce(f32[]{:T(128)} %get-tuple-element.2), channel_id=1, replica_groups=mesh['path'=32,'mp'=2,'period'=4] {'path'}, use_global_device_ids=true, to_apply=%region_7.0 | all-reduce | flops 1 | bytes 8 | tf_op jit(solution)/shard_map/psum | solution.py:51
  484.5 4.6 fusion.15
  489.6 1.5 copy.17
  491.2 144.2 %all-reduce.7.cloned.1.call-done = f32[262144]{0:T(1024)} async-done(((f32[262144]{0:T(1024)}), f32[262144]{0:T(1024)}) %all-reduce.7.cloned.1.call-update) | async-done | bytes 1048592
  635.4 1.4 multiply_reduce_fusion
  636.8 124.7 %psum.53 = f32[]{:T(128)} all-reduce(f32[]{:T(128)} %multiply_reduce_fusion), channel_id=1, replica_groups=mesh['path'=32,'mp'=2,'period'=4] {'path','mp'}, use_global_device_ids=true, to_apply=%region_10.0 | all-reduce | flops 1 | bytes 8 | tf_op jit(solution)/shard_map/psum | solution.py:54
  762.2 0.8 fusion.23
  763.0 0.9 stack.5
  763.9 3.9 reduce.3
  767.9 1.2 reshape.100
  769.1 4.1 all-to-all-start.1
  773.4 16.9 %all-to-all-done.1 = bf16[32,2,4096]{2,1,0:T(2,128)(2,1)S(1)} async-done(((bf16[32,2,4096]{2,1,0:T(2,128)(2,1)}), bf16[32,2,4096]{2,1,0:T(2,128)(2,1)S(1)}, u32[]{:S(2)}, u32[]{:S(2)}) %all-to-all-start.1) | async-done | bytes 524320 | tf_op jit(solution)/shard_map/all_to_all | solution.py:76
  790.7 3.3 reduce.1
  795.0 5.6 fusion.12
  800.8 2.5 psum.54
  804.0 73.2 %psum.55 = f32[]{:T(128)} all-reduce(f32[]{:T(128)} %multiply_reduce_fusion.2), channel_id=1, replica_groups=mesh['path'=32,'mp'=2,'period'=4] {'path'}, use_global_device_ids=true, to_apply=%region_13.0 | all-reduce | flops 1 | bytes 8 | tf_op jit(solution)/shard_map/psum | solution.py:51
  878.6 1.4 multiply_add_fusion
  (41 shorter events, 11.2 us)
Async XLA Ops:
  7.2 87.7 %copy-start.1 = (s32[64]{0:T(128)S(1)}, s32[64]{0:T(128)}, u32[]{:S(2)}) copy-start(s32[64]{0:T(128)} %param.7) | copy-start | bytes 772
  7.2 234.2 %all-reduce.5.cloned.1.call-start = ((), (), s32[]{:S(2)}) async-start(), calls=%async_computation.2 | async-start | bytes 2097152
  90.3 6.8 copy-start.3
  369.9 36.8 %copy-start.2 = (s32[64]{0:T(128)S(1)}, s32[64]{0:T(128)}, u32[]{:S(2)}) copy-start(s32[64]{0:T(128)} %param.6) | copy-start | bytes 772
  370.4 38.9 %copy-start = (f32[2048]{0:T(1024)S(1)}, f32[2048]{0:T(1024)}, u32[]{:S(2)}) copy-start(f32[2048]{0:T(1024)} %param.9) | copy-start | bytes 24580
  375.4 20.9 %all-to-all-start = ((bf16[32,2,4096]{2,1,0:T(2,128)(2,1)}), bf16[32,2,4096]{2,1,0:T(2,128)(2,1)S(1)}, u32[]{:S(2)}, u32[]{:S(2)}) async-start(bf16[32,2,4096]{2,1,0:T(2,128)(2,1)} %reshape.98), calls=%async_computation | async-start | bytes 1048576 | tf_op jit(solution)/shard_map/all_to_all | solution.py:76
  379.3 256.1 %all-reduce.7.cloned.1.call-start = ((), (), s32[]{:S(2)}) async-start(), calls=%async_computation.3 | async-start | bytes 2097152
  769.1 21.2 %all-to-all-start.1 = ((bf16[32,2,4096]{2,1,0:T(2,128)(2,1)}), bf16[32,2,4096]{2,1,0:T(2,128)(2,1)S(1)}, u32[]{:S(2)}, u32[]{:S(2)}) async-start(bf16[32,2,4096]{2,1,0:T(2,128)(2,1)} %reshape.100), calls=%async_computation.1 | async-start | bytes 1048576 | tf_op jit(solution)/shard_map/all_to_all | solution.py:76
Sparse Core Ops, SparseCore 0:
  97.1 144.2 all-reduce.4
  491.3 144.0 all-reduce.6
